TPU v7x, 32 devices: a whole 2x2x4 slice. The times are simulated.
32 devices in a mesh: sec: 4 (over y, x), seq: 8 (over z, core).
Axes of the slice: x: 2, y: 2, z: 4, core: 2. Of those that a mesh axis runs over, the one named last changes fastest.
Arguments:
- long_queries: bfloat16 [16, 4096], P('sec'), may hold values from -15 to 15
- long_keys: bfloat16 [512, 16, 2048], P(('sec', 'seq')), may hold values from -6 to 6
- long_values: bfloat16 [512, 16, 2048], P(('sec', 'seq')), may hold values from -6 to 6
- page_table: int32 [16, 32], replicated, may hold values from 0 to 511, as said below
- long_lengths: int32 [16], replicated, may hold values from 1 to 512, 5120 in all
- short_queries: bfloat16 [32, 256], P(('sec', 'seq')), may hold values from -15 to 15
- short_keys: bfloat16 [32, 2048, 128], P(('sec', 'seq')), may hold values from -6 to 6
- short_values: bfloat16 [32, 2048, 128], P(('sec', 'seq')), may hold values from -6 to 6
- short_lengths: int32 [2], replicated, may hold values from 1 to 2048, 2560 in all
- out_weight: bfloat16 [4096, 4608], P('seq', 'sec'), may hold values from -0.09375 to 0.09375
- long_resid: bfloat16 [16, 4608], P(None, 'sec'), may hold values from -1.5 to 1.5
Outputs:
- long_out: bfloat16 [16, 4608], P(None, 'sec')
- short_out: bfloat16 [32, 256], P(('sec', 'seq'))
Inputs may be any that keep to these rules, and one draw needn't show every extreme that they name: `page_table`: row r lists the 32 pool pages of long request r in order of position; every page of the pool of 512 appears exactly once; page g is held by device g // 16 along sec+seq. `long_lengths`: counts the newest token; later slots are unused. `short_lengths`: counts the newest token; later slots are unused.
All inputs are finite; a program needn't handle non-finite values.
Results may differ from a plain program's by a relative error of at most 0.0055.
Values may be sent and summed in bfloat16 or wider, within the bound.
A program may use at most 64 MiB of HBM per device.

v0:
```python
import jax
import jax.numpy as jnp
from jax import lax
from jax.sharding import PartitionSpec as P

KVH = 16
HD = 128
G = 2
soft_cap = 50.0
score_scale = 144.0 ** (-0.5)


def capped_weights(raw_scores, live_mask):
    capped = soft_cap * jnp.tanh(raw_scores * (score_scale / soft_cap))
    return jnp.where(live_mask, jnp.exp(capped), 0.0)


def per_device(
    long_queries,
    long_keys,
    long_values,
    page_table,
    long_lengths,
    short_queries,
    short_keys,
    short_values,
    short_lengths,
    out_weight,
    long_resid,
):
    queries = lax.all_gather(long_queries, "sec", axis=0, tiled=True)
    requests = queries.shape[0]
    page_count, page_len, kv_width = long_keys.shape
    tokens = page_count * page_len
    head_count = KVH * G
    first_page = lax.axis_index(("sec", "seq")) * page_count
    page_ids = first_page + jnp.arange(page_count, dtype=jnp.int32)
    matched = page_table[:, :, None] == page_ids[None, None, :]
    page_held = jnp.any(matched, axis=1)
    slot_index = jnp.arange(page_table.shape[1], dtype=jnp.int32)
    slot_of = jnp.sum(jnp.where(matched, slot_index[None, :, None], 0), axis=1)
    position = slot_of[:, :, None] * page_len + jnp.arange(page_len, dtype=jnp.int32)[None, None, :]
    live_mask = page_held[:, :, None] & (position < long_lengths[:, None, None])
    live_mask = live_mask.reshape(requests, tokens)
    grouped = (
        queries.reshape(requests, KVH, G, HD).transpose(1, 0, 2, 3).reshape(KVH, requests * G, HD)
    )
    key_rows = long_keys.reshape(tokens, KVH, HD)
    value_rows = long_values.reshape(tokens, KVH, HD)
    raw_scores = jnp.einsum("hqd,thd->hqt", grouped, key_rows, preferred_element_type=jnp.float32)
    token_mask = jnp.broadcast_to(live_mask[None, :, None, :], (KVH, requests, G, tokens)).reshape(
        KVH, requests * G, tokens
    )
    weights = capped_weights(raw_scores, token_mask)
    totals = jnp.sum(weights, axis=2)
    part_sums = jnp.einsum(
        "hqt,thd->hqd", weights.astype(jnp.bfloat16), value_rows, preferred_element_type=jnp.float32
    )
    part_sums = (
        part_sums.reshape(KVH, requests, G, HD)
        .transpose(1, 0, 2, 3)
        .reshape(requests, head_count * HD)
    )
    totals = totals.reshape(KVH, requests, G).transpose(1, 0, 2).reshape(requests, head_count)
    share_width = out_weight.shape[0]
    share_start = lax.axis_index("seq") * share_width
    part_sums, totals = lax.psum((part_sums, totals), ("sec", "seq"))
    attention = (
        (part_sums.reshape(requests, head_count, HD) / totals[:, :, None])
        .astype(jnp.bfloat16)
        .reshape(requests, head_count * HD)
    )
    feature_rows = lax.dynamic_slice_in_dim(attention, share_start, share_width, 1)
    partial_proj = jnp.dot(feature_rows, out_weight, preferred_element_type=jnp.float32)
    projected = lax.psum(partial_proj, "seq")
    long_out = (long_resid.astype(jnp.float32) + projected).astype(jnp.bfloat16)
    pair_count = short_queries.shape[0]
    length = short_keys.shape[1]
    pair_ids = lax.axis_index(("sec", "seq")) * pair_count + jnp.arange(pair_count, dtype=jnp.int32)
    request_of = pair_ids // KVH
    chosen = request_of[:, None] == jnp.arange(short_lengths.shape[0], dtype=jnp.int32)[None, :]
    pair_limit = jnp.sum(jnp.where(chosen, short_lengths[None, :], 0), axis=1)
    short_live = jnp.arange(length, dtype=jnp.int32)[None, :] < pair_limit[:, None]
    pair_queries = short_queries.reshape(pair_count, G, HD)
    short_scores = jnp.einsum(
        "pgd,ptd->pgt", pair_queries, short_keys, preferred_element_type=jnp.float32
    )
    short_weights = capped_weights(short_scores, short_live[:, None, :])
    short_totals = jnp.sum(short_weights, axis=2)
    short_sums = jnp.einsum(
        "pgt,ptd->pgd",
        short_weights.astype(jnp.bfloat16),
        short_values,
        preferred_element_type=jnp.float32,
    )
    short_out = (
        (short_sums / short_totals[:, :, None]).astype(jnp.bfloat16).reshape(pair_count, G * HD)
    )
    return (long_out, short_out)


def solution(mesh):
    in_specs = (
        P("sec", None),
        P(("sec", "seq"), None, None),
        P(("sec", "seq"), None, None),
        P(),
        P(),
        P(("sec", "seq"), None),
        P(("sec", "seq"), None, None),
        P(("sec", "seq"), None, None),
        P(),
        P("seq", "sec"),
        P(None, "sec"),
    )
    out_specs = (P(None, "sec"), P(("sec", "seq"), None))
    return jax.shard_map(
        per_device, mesh=mesh, in_specs=in_specs, out_specs=out_specs, check_vma=False
    )
```

profile of v0, /device:TPU:8, one launch (start us, length us, event | category | flops | bytes accessed | tf_op | source)
XLA Modules:
  0.0 212.9 jit_solution(14925022806387552283)
XLA Ops:
  7.2 0.0 copy-start
  7.2 0.0 all-reduce.3.cloned.1.call-start
  7.2 1.2 fusion.16
  8.4 1.1 compare_reduce_fusion
  9.6 0.1 add.56
  9.7 0.0 copy-start.4
  9.7 0.1 add.57
  9.8 0.1 and.21
  9.9 0.1 and.22
  10.0 0.1 add.59
  10.1 0.7 fusion.20
  10.9 0.0 copy-start.1
  10.9 1.5 copy.36
  12.5 0.0 copy-done.4
  12.5 8.5 %all-gather = bf16[4,4,4096]{2,1,0:T(4,128)(2,1)S(1)} all-gather(bf16[1,4,4096]{2,1,0:T(4,128)(2,1)S(1)} %bitcast.58), channel_id=1, replica_groups=mesh['sec'=4,'seq'=8] {'sec'}, dimensions={0}, use_global_device_ids=true | all-gather | bytes 163840 | tf_op jit(solution)/shard_map/all_gather | solution.py:31
  20.9 0.2 reshape.129
  21.1 0.1 copy.29
  21.2 0.0 copy-done.1
  21.2 0.2 copy.37
  21.4 0.6 fusion.25
  22.0 0.3 fusion.10
  22.4 0.0 copy-start.5
  22.4 0.0 copy-start.2
  22.4 0.1 copy.50
  22.5 0.9 reshape.134
  23.4 0.0 all-reduce.3.cloned.1.call-update
  23.5 0.0 all-reduce.5.cloned.1.call-start
  23.5 0.0 copy-done.7
  23.5 0.6 fusion.22
  24.2 0.7 iota_compare_fusion
  24.8 0.1 copy.33
  24.9 0.1 copy.34
  25.0 39.6 %psum.22 = f32[16,32]{0,1:T(8,128)S(1)} all-reduce(f32[16,32]{0,1:T(8,128)S(1)} %bitcast.57), channel_id=1, replica_groups=mesh['sec'=4,'seq'=8] {'sec','seq'}, use_global_device_ids=true, to_apply=%region_4.5 | all-reduce | flops 512 | bytes 4096 | tf_op jit(solution)/shard_map/psum | solution.py:67
  64.6 0.1 copy.35
  64.7 0.1 div.30
  64.8 0.0 copy-start.6
  64.8 0.2 copy.49
  65.0 0.0 copy-done.5
  65.0 0.0 copy-done.2
  65.0 0.0 copy-start.3
  65.0 0.4 fusion.26
  65.4 85.0 %all-reduce.3.cloned.1.call-done = f32[16,4096]{1,0:T(8,128)} async-done(((f32[16,4096]{1,0:T(8,128)}), f32[16,4096]{1,0:T(8,128)}) %all-reduce.3.cloned.1.call-update) | async-done | bytes 262160 | tf_op jit(solution)/shard_map/psum | solution.py:67
  150.4 1.6 fusion.18
  152.1 0.0 all-reduce.5.cloned.1.call-update
  152.1 0.2 fusion.9
  152.3 0.6 copy.51
  152.9 51.7 %all-reduce.5.cloned.1.call-done = f32[16,1152]{1,0:T(8,128)} async-done(((f32[16,1152]{1,0:T(8,128)}), f32[16,1152]{1,0:T(8,128)}) %all-reduce.5.cloned.1.call-update) | async-done | bytes 73744 | tf_op jit(solution)/shard_map/psum | solution.py:75
  204.5 1.5 add_convert_fusion
  (10 shorter events, 0.1 us)
Async XLA Ops:
  7.2 143.3 %copy-start = (bf16[512,1152]{1,0:T(8,128)(2,1)S(1)}, bf16[512,1152]{1,0:T(8,128)(2,1)}, u32[]{:S(2)}) copy-start(bf16[512,1152]{1,0:T(8,128)(2,1)} %param.20) | copy-start | bytes 3538948
  7.2 143.2 %all-reduce.3.cloned.1.call-start = ((), (), s32[]{:S(2)}) async-start(), calls=%async_computation | async-start | bytes 524288 | tf_op jit(solution)/shard_map/psum | solution.py:67
  9.7 2.8 %copy-start.4 = (bf16[4,4096]{1,0:T(4,128)(2,1)S(1)}, bf16[4,4096]{1,0:T(4,128)(2,1)}, u32[]{:S(2)}) copy-start(bf16[4,4096]{1,0:T(4,128)(2,1)} %param.11) | copy-start | bytes 98308
  10.9 10.3 %copy-start.1 = (bf16[16,16,2048]{2,1,0:T(8,128)(2,1)S(1)}, bf16[16,16,2048]{2,1,0:T(8,128)(2,1)}, u32[]{:S(2)}) copy-start(bf16[16,16,2048]{2,1,0:T(8,128)(2,1)} %param.13) | copy-start | bytes 3145732
  22.0 1.5 copy-start.7
  22.4 42.6 %copy-start.5 = (bf16[1,256]{1,0:T(2,128)(2,1)S(1)}, bf16[1,256]{1,0:T(2,128)(2,1)}, u32[]{:S(2)}) copy-start(bf16[1,256]{1,0:T(2,128)(2,1)} %param.16) | copy-start | bytes 1540
  22.4 42.6 %copy-start.2 = (bf16[1,2048,128]{2,1,0:T(8,128)(2,1)S(1)}, bf16[1,2048,128]{2,1,0:T(8,128)(2,1)}, u32[]{:S(2)}) copy-start(bf16[1,2048,128]{2,1,0:T(8,128)(2,1)} %param.17) | copy-start | bytes 1572868
  23.5 181.1 %all-reduce.5.cloned.1.call-start = ((), (), s32[]{:S(2)}) async-start(), calls=%async_computation.1 | async-start | bytes 147456 | tf_op jit(solution)/shard_map/psum | solution.py:75
  64.8 87.3 %copy-start.6 = (bf16[1,2048,128]{2,1,0:T(8,128)(2,1)S(1)}, bf16[1,2048,128]{2,1,0:T(8,128)(2,1)}, u32[]{:S(2)}) copy-start(bf16[1,2048,128]{2,1,0:T(8,128)(2,1)} %param.18) | copy-start | bytes 1572868
  65.0 139.5 %copy-start.3 = (bf16[16,1152]{1,0:T(8,128)(2,1)S(1)}, bf16[16,1152]{1,0:T(8,128)(2,1)}, u32[]{:S(2)}) copy-start(bf16[16,1152]{1,0:T(8,128)(2,1)} %param.21) | copy-start | bytes 110596
Sparse Core Ops, SparseCore 0:
  23.6 126.7 all-reduce.2
  152.8 51.7 all-reduce.4
where the time goes:
time: 213 us
  waiting for transfers between devices  137 us (64%)
  blocking collectives  48.1 us (23%)
  between operations  14.3 us (7%)
  other arithmetic  5.86 us (3%)
  local copies, waits for them, and re-layouts  4.75 us (2%)
  matrix products  3.13 us (1%)
    psum x1, waiting for transfers between devices, per_device(): part_sums, totals = lax.psum((part_sums, totals), ('sec', 'seq'))  85 us
    psum x1, waiting for transfers between devices, per_device(): projected = lax.psum(partial_proj, 'seq')  51.7 us
    psum x1, blocking collectives, per_device(): part_sums, totals = lax.psum((part_sums, totals), ('sec', 'seq'))  39.6 us
    all_gather x1, blocking collectives, per_device(): queries = lax.all_gather(long_queries, 'sec', axis=0, tiled=True)  8.46 us
  transfers between devices with their start and end apart: 2, of which 2 were waited for; matrix products, arithmetic and copies ran while one was open for 1% of the time, Pallas kernels for 0%

commit v1 on v0

--- a/solution.py
+++ b/solution.py
@@ -72,7 +72,7 @@
     )
     feature_rows = lax.dynamic_slice_in_dim(attention, share_start, share_width, 1)
     partial_proj = jnp.dot(feature_rows, out_weight, preferred_element_type=jnp.float32)
-    projected = lax.psum(partial_proj, "seq")
+    projected = jnp.sum(lax.all_gather(partial_proj, "seq"), axis=0)
     long_out = (long_resid.astype(jnp.float32) + projected).astype(jnp.bfloat16)
     pair_count = short_queries.shape[0]
     length = short_keys.shape[1]

time: 213 us -> 176 us (0.83); the launches traced: 213 us -> 173 us
  waiting for transfers between devices: 137 us -> 84.6 us
  blocking collectives: 48.1 us -> 62 us
    psum x1 -> x0, waiting for transfers between devices: 51.7 us -> none  [per_device(): projected = lax.psum(partial_proj, 'seq')]
    all_gather x0 -> x1, blocking collectives: none -> 14 us  [per_device(): projected = jnp.sum(lax.all_gather(partial_proj, 'seq'), axis=0)]
  transfers between devices with their start and end apart: 2 -> 1, of which waited for: 2 -> 1; matrix products, arithmetic and copies ran while one was open for 1% -> 2% of each run, Pallas kernels for 0% -> 0%
where the time goes in v1:
time: 176 us; the launch traced here: 173 us
  waiting for transfers between devices  84.6 us (48%)
  blocking collectives  62 us (35%)
  between operations  14.3 us (8%)
  other arithmetic  5.01 us (3%)
  local copies, waits for them, and re-layouts  4.75 us (3%)
  matrix products  2.5 us (1%)
    psum x1, waiting for transfers between devices, per_device(): part_sums, totals = lax.psum((part_sums, totals), ('sec', 'seq'))  84.6 us
    psum x1, blocking collectives, per_device(): part_sums, totals = lax.psum((part_sums, totals), ('sec', 'seq'))  39.5 us
    all_gather x1, blocking collectives, per_device(): projected = jnp.sum(lax.all_gather(partial_proj, 'seq'), axis=0)  14 us
    all_gather x1, blocking collectives, per_device(): queries = lax.all_gather(long_queries, 'sec', axis=0, tiled=True)  8.46 us
  transfers between devices with their start and end apart: 1, of which 1 were waited for; matrix products, arithmetic and copies ran while one was open for 2% of the time, Pallas kernels for 0%

profile of v1, /device:TPU:8, one launch (start us, length us, event | category | flops | bytes accessed | tf_op | source)
XLA Modules:
  0.0 173.1 jit_solution(6206598683913826333)
XLA Ops:
  7.2 0.0 copy-start
  7.2 0.0 all-reduce.2.cloned.1.call-start
  7.2 1.2 fusion.16
  8.4 1.1 compare_reduce_fusion
  9.6 0.1 add.54
  9.7 0.0 copy-start.4
  9.7 0.1 add.55
  9.8 0.1 and.21
  9.9 0.1 and.22
  10.0 0.1 add.57
  10.1 0.7 fusion.20
  10.9 0.0 copy-start.1
  10.9 1.5 copy.36
  12.5 0.0 copy-done.4
  12.5 8.5 %all-gather.1 = bf16[4,4,4096]{2,1,0:T(4,128)(2,1)S(1)} all-gather(bf16[1,4,4096]{2,1,0:T(4,128)(2,1)S(1)} %bitcast.60), channel_id=1, replica_groups=mesh['sec'=4,'seq'=8] {'sec'}, dimensions={0}, use_global_device_ids=true | all-gather | bytes 163840 | tf_op jit(solution)/shard_map/all_gather | solution.py:31
  20.9 0.2 reshape.129
  21.1 0.1 copy.29
  21.2 0.0 copy-done.1
  21.2 0.2 copy.37
  21.4 0.6 fusion.25
  22.0 0.0 copy-start.7
  22.0 0.0 copy-start.2
  22.0 0.3 fusion.10
  22.4 0.0 copy-start.6
  22.4 0.1 copy.50
  22.5 0.9 reshape.134
  23.4 0.0 all-reduce.2.cloned.1.call-update
  23.5 0.0 copy-done.7
  23.5 0.6 fusion.22
  24.1 0.7 iota_compare_fusion
  24.8 0.0 copy-done.5
  24.8 0.0 copy-done.2
  24.8 0.4 fusion.26
  25.2 0.0 copy-done.6
  25.2 0.2 fusion.9
  25.4 0.6 copy.51
  26.0 0.1 copy.33
  26.0 0.1 copy.34
  26.1 39.5 %psum.15 = f32[16,32]{0,1:T(8,128)S(1)} all-reduce(f32[16,32]{0,1:T(8,128)S(1)} %bitcast.59), channel_id=1, replica_groups=mesh['sec'=4,'seq'=8] {'sec','seq'}, use_global_device_ids=true, to_apply=%region_4.5 | all-reduce | flops 512 | bytes 4096 | tf_op jit(solution)/shard_map/psum | solution.py:67
  65.6 0.1 copy.35
  65.7 0.1 div.30
  65.8 0.2 copy.49
  66.0 84.6 %all-reduce.2.cloned.1.call-done = f32[16,4096]{1,0:T(8,128)} async-done(((f32[16,4096]{1,0:T(8,128)}), f32[16,4096]{1,0:T(8,128)}) %all-reduce.2.cloned.1.call-update) | async-done | bytes 262160 | tf_op jit(solution)/shard_map/psum | solution.py:67
  150.5 0.0 copy-done
  150.5 1.0 fusion.18
  151.6 14.0 %all-gather = f32[128,1152]{1,0:T(8,128)S(1)} all-gather(f32[16,1152]{1,0:T(8,128)S(1)} %fusion.18), channel_id=2, replica_groups=mesh['sec'=4,'seq'=8] {'seq'}, dimensions={0}, use_global_device_ids=true | all-gather | bytes 663552 | tf_op jit(solution)/shard_map/all_gather | solution.py:75
  165.6 0.0 copy-done.3
  165.6 0.6 add_convert_fusion
  (9 shorter events, 0.1 us)
Async XLA Ops:
  7.2 143.4 %copy-start = (bf16[512,1152]{1,0:T(8,128)(2,1)S(1)}, bf16[512,1152]{1,0:T(8,128)(2,1)}, u32[]{:S(2)}) copy-start(bf16[512,1152]{1,0:T(8,128)(2,1)} %param.20) | copy-start | bytes 3538948
  7.2 143.4 %all-reduce.2.cloned.1.call-start = ((), (), s32[]{:S(2)}) async-start(), calls=%async_computation | async-start | bytes 524288 | tf_op jit(solution)/shard_map/psum | solution.py:67
  9.7 2.8 %copy-start.4 = (bf16[4,4096]{1,0:T(4,128)(2,1)S(1)}, bf16[4,4096]{1,0:T(4,128)(2,1)}, u32[]{:S(2)}) copy-start(bf16[4,4096]{1,0:T(4,128)(2,1)} %param.11) | copy-start | bytes 98308
  10.9 10.3 %copy-start.1 = (bf16[16,16,2048]{2,1,0:T(8,128)(2,1)S(1)}, bf16[16,16,2048]{2,1,0:T(8,128)(2,1)}, u32[]{:S(2)}) copy-start(bf16[16,16,2048]{2,1,0:T(8,128)(2,1)} %param.13) | copy-start | bytes 3145732
  22.0 1.5 copy-start.7
  22.0 2.8 %copy-start.5 = (bf16[1,256]{1,0:T(2,128)(2,1)S(1)}, bf16[1,256]{1,0:T(2,128)(2,1)}, u32[]{:S(2)}) copy-start(bf16[1,256]{1,0:T(2,128)(2,1)} %param.16) | copy-start | bytes 1540
  22.0 2.8 %copy-start.2 = (bf16[1,2048,128]{2,1,0:T(8,128)(2,1)S(1)}, bf16[1,2048,128]{2,1,0:T(8,128)(2,1)}, u32[]{:S(2)}) copy-start(bf16[1,2048,128]{2,1,0:T(8,128)(2,1)} %param.17) | copy-start | bytes 1572868
  22.4 2.8 %copy-start.6 = (bf16[1,2048,128]{2,1,0:T(8,128)(2,1)S(1)}, bf16[1,2048,128]{2,1,0:T(8,128)(2,1)}, u32[]{:S(2)}) copy-start(bf16[1,2048,128]{2,1,0:T(8,128)(2,1)} %param.18) | copy-start | bytes 1572868
  150.5 15.1 %copy-start.3 = (bf16[16,1152]{1,0:T(8,128)(2,1)S(1)}, bf16[16,1152]{1,0:T(8,128)(2,1)}, u32[]{:S(2)}) copy-start(bf16[16,1152]{1,0:T(8,128)(2,1)} %param.21) | copy-start | bytes 110596
Sparse Core Ops, SparseCore 0:
  23.6 126.9 all-reduce.1
